TPU v7x, 128 devices: a whole 4x4x4 slice. The times are simulated.
128 devices in a mesh: dp: 8 (over z_lo, x), seq: 16 (over z_hi, y, core).
Axes of the slice: x: 4, y: 4, z: 4 (z_hi: 2, z_lo: 2; z = z_hi * 2 + z_lo), core: 2. Of those that a mesh axis runs over, the one named last changes fastest.
Arguments:
- series: bfloat16 [8, 8192, 128], P('dp', 'seq'), may hold values from -6 to 6
- cotangent: bfloat16 [8, 8192, 128], P('dp', 'seq'), may hold values from -6 to 6
- w_in: bfloat16 [128, 384], replicated, may hold values from -0.5 to 0.5
- w_out: bfloat16 [128, 128], replicated, may hold values from -0.5 to 0.5
- taps: float32 [3, 384], replicated, may hold values from -3 to 3
- skip_one: float32 [128], replicated, may hold values from 0.5 to 1.5
- skip_two: float32 [128], replicated, may hold values from 0.5 to 1.5
- filter_one: float32 [8, 8192], P(None, 'seq'), may hold values from -0.0625 to 0.0625
- filter_two: float32 [8, 8192], P(None, 'seq'), may hold values from -0.0625 to 0.0625
Outputs:
- output: bfloat16 [8, 8192, 128], P('dp', 'seq')
- d_series: bfloat16 [8, 8192, 128], P('dp', 'seq')
- grad_w_in: float32 [128, 384], replicated
- grad_w_out: float32 [128, 128], replicated
- grad_taps: float32 [3, 384], replicated
- grad_skip_one: float32 [128], replicated
- grad_skip_two: float32 [128], replicated
- grad_filter_one: float32 [8, 8192], P(None, 'seq')
- grad_filter_two: float32 [8, 8192], P(None, 'seq')
All inputs are finite; a program needn't handle non-finite values.
Results may differ from a plain program's by a relative error of at most 0.015.
Values may be sent and summed in bfloat16 or wider, within the bound.
A program may use at most 128 MiB of HBM per device.

v0:
```python
import math
import numpy as np
import jax
import jax.numpy as jnp
from jax import lax
from jax.sharding import PartitionSpec as P

HIGHEST = lax.Precision.HIGHEST
LANES = 128


def dft_tables(length):
    size = 2 * length
    rows = size // LANES
    half = length // LANES
    k1 = np.arange(rows)
    f1 = np.exp(-2j * np.pi * (np.outer(k1, np.arange(half)) % rows) / rows)
    turn = np.exp(-2j * np.pi * np.outer(k1, np.arange(LANES)) / size)
    f2 = np.exp(-2j * np.pi * (np.outer(np.arange(LANES), np.arange(LANES)) % LANES) / LANES)
    fwd1 = np.concatenate([f1.real, f1.imag], axis=0)
    fwd2 = np.block([[f2.real, f2.imag], [-f2.imag, f2.real]])
    inv2 = np.block([[f2.real, -f2.imag], [f2.imag, f2.real]])
    inv1 = np.concatenate([f1.real.T, f1.imag.T], axis=1) / size
    as32 = lambda a: jnp.asarray(np.asarray(a, np.float32))
    return {
        "rows": rows,
        "fwd1": as32(fwd1),
        "fwd2": as32(fwd2),
        "inv1": as32(inv1),
        "inv2": as32(inv2),
        "turn_r": as32(turn.real)[:, None, :],
        "turn_i": as32(turn.imag)[:, None, :],
    }


def spectrum(x, tab):
    rows = tab["rows"]
    a = jnp.einsum("kn,ncm->kcm", tab["fwd1"], x, precision=HIGHEST)
    ar, ai = (a[:rows], a[rows:])
    tr, ti = (tab["turn_r"], tab["turn_i"])
    cat = jnp.concatenate([ar * tr - ai * ti, ar * ti + ai * tr], axis=-1)
    return jnp.einsum("kcm,mj->kcj", cat, tab["fwd2"], precision=HIGHEST)


def signal(s, tab):
    b = jnp.einsum("kcj,jm->kcm", s, tab["inv2"], precision=HIGHEST)
    br, bi = (b[..., :LANES], b[..., LANES:])
    tr, ti = (tab["turn_r"], tab["turn_i"])
    stacked = jnp.concatenate([br * tr + bi * ti, bi * tr - br * ti], axis=0)
    return jnp.einsum("nk,kcm->ncm", tab["inv1"], stacked, precision=HIGHEST)


def cmul(a, b, conj=False):
    ar, ai = (a[..., :LANES], a[..., LANES:])
    br, bi = (b[..., :LANES], b[..., LANES:])
    if conj:
        bi = -bi
    return jnp.concatenate([ar * br - ai * bi, ar * bi + ai * br], axis=-1)


def fold(x):
    c, length = x.shape
    return jnp.swapaxes(x.reshape(c, length // LANES, LANES), 0, 1)


def unfold(x):
    half, c, lanes = x.shape
    return jnp.swapaxes(x, 0, 1).reshape(c, half * lanes)


def shards(series, cotangent, w_in, w_out, taps, skip_one, skip_two, filter_one, filter_two):
    _, block, width = series.shape
    seq_n = lax.axis_size("seq")
    dp_n = lax.axis_size("dp")
    length = block * seq_n
    half = length // LANES
    me = lax.axis_index("seq")
    per = width // seq_n
    filters = filter_one.shape[0]
    group_width = width // filters
    per_group = group_width // per
    group = me // per_group
    grad_scale = 1.0 / math.sqrt(dp_n * series.shape[0] * length)
    tab = dft_tables(length)
    rows_sent = jnp.repeat(
        jnp.swapaxes(jnp.stack([filter_one, filter_two]), 0, 1), per_group, axis=0
    )
    rows_got = lax.all_to_all(rows_sent, "seq", 0, 0, tiled=True)
    h_rows = jnp.swapaxes(rows_got, 0, 1).reshape(2, length)
    taps_sel = lax.dynamic_index_in_dim(
        taps.reshape(3, 3, seq_n, per), me, axis=2, keepdims=False
    ).reshape(3, 3 * per)
    skip1 = lax.dynamic_index_in_dim(skip_one.reshape(seq_n, per), me, axis=0, keepdims=False)
    skip2 = lax.dynamic_index_in_dim(skip_two.reshape(seq_n, per), me, axis=0, keepdims=False)
    skip1 = skip1[None, :, None]
    skip2 = skip2[None, :, None]
    proj_blk = jnp.einsum("td,dc->ct", series[0], w_in, preferred_element_type=jnp.float32)
    proj_blk = lax.all_to_all(proj_blk.reshape(3, seq_n, per, block), "seq", 1, 1, tiled=True)
    proj = jnp.swapaxes(proj_blk, 1, 2).reshape(3 * per, length)
    prev1 = jnp.pad(proj, ((0, 0), (1, 0)))[:, :length]
    prev2 = jnp.pad(proj, ((0, 0), (2, 0)))[:, :length]
    conv = taps_sel[0][:, None] * proj + taps_sel[1][:, None] * prev1 + taps_sel[2][:, None] * prev2
    conv_f = fold(conv)
    value = conv_f[:, :per]
    gate_one = conv_f[:, per : 2 * per]
    gate_two = conv_f[:, 2 * per :]
    h_spec = spectrum(fold(h_rows), tab)
    h_one = h_spec[:, 0:1]
    h_two = h_spec[:, 1:2]
    v_spec = spectrum(value, tab)
    y_one = signal(cmul(v_spec, h_one), tab) + skip1 * value
    gated_mid = gate_one * y_one
    m_spec = spectrum(gated_mid, tab)
    y_two = signal(cmul(m_spec, h_two), tab) + skip2 * gated_mid
    product = (gate_two * y_two).astype(jnp.bfloat16)
    dprod_blk = jnp.einsum("td,cd->ct", cotangent[0], w_out, preferred_element_type=jnp.float32)
    dprod_blk = lax.all_to_all(dprod_blk.reshape(seq_n, per, block), "seq", 0, 0, tiled=True)
    d_product = jnp.swapaxes(dprod_blk.reshape(seq_n, per, block // LANES, LANES), 1, 2).reshape(
        half, per, LANES
    )
    grad_two = d_product * gate_two
    d_gate_two = d_product * y_two
    g2_spec = spectrum(grad_two, tab)
    d_mid = signal(cmul(g2_spec, h_two, conj=True), tab) + skip2 * grad_two
    grad_one = d_mid * gate_one
    d_gate_one = d_mid * y_one
    g1_spec = spectrum(grad_one, tab)
    d_value = signal(cmul(g1_spec, h_one, conj=True), tab) + skip1 * grad_one
    corr = jnp.concatenate(
        [
            jnp.sum(cmul(g1_spec, v_spec, conj=True), axis=1, keepdims=True),
            jnp.sum(cmul(g2_spec, m_spec, conj=True), axis=1, keepdims=True),
        ],
        axis=1,
    )
    filt_grad = unfold(signal(corr, tab))
    d_conv = unfold(jnp.concatenate([d_value, d_gate_one, d_gate_two], axis=1))
    next1 = jnp.pad(d_conv, ((0, 0), (0, 1)))[:, 1:]
    next2 = jnp.pad(d_conv, ((0, 0), (0, 2)))[:, 2:]
    d_proj = (
        taps_sel[0][:, None] * d_conv + taps_sel[1][:, None] * next1 + taps_sel[2][:, None] * next2
    ).astype(jnp.bfloat16)
    local_taps = jnp.stack(
        [
            jnp.sum(d_conv * proj, axis=1),
            jnp.sum(d_conv * prev1, axis=1),
            jnp.sum(d_conv * prev2, axis=1),
        ]
    )
    local_skip1 = jnp.sum(grad_one * value, axis=(0, 2))
    local_skip2 = jnp.sum(grad_two * gated_mid, axis=(0, 2))
    prod_blocks = product.reshape(seq_n, half // seq_n, per, LANES)
    prod_blocks = lax.all_to_all(prod_blocks, "seq", 0, 0, tiled=True)
    output = jnp.einsum(
        "jnim,jid->nmd",
        prod_blocks,
        w_out.reshape(seq_n, per, width),
        preferred_element_type=jnp.float32,
    ).astype(jnp.bfloat16)
    output = output.reshape(1, block, width)
    dp_blocks = d_proj.reshape(3, per, seq_n, block)
    dp_blocks = lax.all_to_all(dp_blocks, "seq", 2, 2, tiled=True)
    d_series = jnp.einsum(
        "pijt,dpji->td",
        dp_blocks,
        w_in.reshape(width, 3, seq_n, per),
        preferred_element_type=jnp.float32,
    ).astype(jnp.bfloat16)
    d_series = d_series.reshape(1, block, width)
    fg_blocks = lax.all_to_all(filt_grad.reshape(2, seq_n, block), "seq", 1, 1, tiled=True)
    fg_blocks = jnp.sum(fg_blocks.reshape(2, filters, per_group, block), axis=2)
    prod_rows = jnp.transpose(prod_blocks, (1, 3, 0, 2)).reshape(block, width)
    dp_rows = jnp.transpose(dp_blocks, (3, 0, 2, 1)).reshape(block, 3 * width)
    local_w_in = jnp.einsum("td,tc->dc", series[0], dp_rows, preferred_element_type=jnp.float32)
    local_w_out = jnp.einsum(
        "tc,td->cd", prod_rows, cotangent[0], preferred_element_type=jnp.float32
    )
    small = jnp.concatenate(
        [
            local_taps.reshape(3, 3, 1, per),
            jnp.stack([local_skip1, local_skip2, jnp.zeros_like(local_skip1)]).reshape(
                3, 1, 1, per
            ),
        ],
        axis=1,
    )
    small_full = jnp.zeros((3, 4, seq_n, per), jnp.float32)
    small_full = lax.dynamic_update_slice(small_full, small, (0, 0, me, 0))
    grad_w_in, grad_w_out, small_full = lax.psum(
        (local_w_in, local_w_out, small_full), ("dp", "seq")
    )
    fg_blocks = lax.psum(fg_blocks, "dp")
    small_full = small_full.reshape(3, 4, width)
    grad_taps = small_full[:, :3].reshape(3, 3 * width)
    grad_skip_one = small_full[0, 3]
    grad_skip_two = small_full[1, 3]
    return (
        output,
        d_series,
        grad_scale * grad_w_in,
        grad_scale * grad_w_out,
        grad_scale * grad_taps,
        grad_scale * grad_skip_one,
        grad_scale * grad_skip_two,
        grad_scale * fg_blocks[0],
        grad_scale * fg_blocks[1],
    )


def solution(mesh):
    in_specs = (
        P("dp", "seq", None),
        P("dp", "seq", None),
        P(),
        P(),
        P(),
        P(),
        P(),
        P(None, "seq"),
        P(None, "seq"),
    )
    out_specs = (
        P("dp", "seq", None),
        P("dp", "seq", None),
        P(),
        P(),
        P(),
        P(),
        P(),
        P(None, "seq"),
        P(None, "seq"),
    )
    return jax.shard_map(shards, mesh=mesh, in_specs=in_specs, out_specs=out_specs, check_vma=False)
```

profile of v0, /device:TPU:1, one launch (start us, length us, event | category | flops | bytes accessed | tf_op | source)
XLA Modules:
  0.0 364.3 jit_solution(12172871343249868817)
XLA Ops:
  7.2 0.8 maximum_bitcast_fusion
  8.0 0.6 broadcast_in_dim.16
  8.6 9.4 %all-to-all-start.1 = ((f32[16,2,512]{2,1,0:T(2,128)}), f32[16,2,512]{2,1,0:T(2,128)S(1)}, u32[]{:S(2)}, u32[]{:S(2)}) async-start(f32[16,2,512]{2,1,0:T(2,128)} %bitcast.12), calls=%async_computation.1 | async-start | bytes 131072 | tf_op jit(solution)/shard_map/all_to_all | solution.py:88
  18.1 0.7 copy-done.11
  20.6 1.2 fusion.68
  21.8 0.9 fusion.70
  22.7 2.7 all-to-all-done.1
  25.4 4.6 %all-to-all-start.3 = ((f32[16,8,512]{2,1,0:T(8,128)}), f32[16,8,512]{2,1,0:T(8,128)S(1)}, u32[]{:S(2)}, u32[]{:S(2)}) async-start(f32[16,8,512]{2,1,0:T(8,128)} %fusion.70), calls=%async_computation.3 | async-start | bytes 524288 | tf_op jit(solution)/shard_map/all_to_all | solution.py:117
  30.0 0.8 copy-done.6
  31.8 6.9 %all-to-all-done.3 = f32[16,8,512]{2,1,0:T(8,128)S(1)} async-done(((f32[16,8,512]{2,1,0:T(8,128)}), f32[16,8,512]{2,1,0:T(8,128)S(1)}, u32[]{:S(2)}, u32[]{:S(2)}) %all-to-all-start.3) | async-done | bytes 262176 | tf_op jit(solution)/shard_map/all_to_all | solution.py:117
  38.7 4.2 %all-to-all-start = ((f32[3,16,8,512]{3,2,0,1:T(8,128)}), f32[3,16,8,512]{3,2,0,1:T(8,128)S(1)}, u32[]{:S(2)}, u32[]{:S(2)}) async-start(f32[3,16,8,512]{3,2,0,1:T(8,128)} %fusion.68), calls=%async_computation | async-start | bytes 1572864 | tf_op jit(solution)/shard_map/all_to_all | solution.py:98
  43.6 13.9 %all-to-all-done = f32[3,16,8,512]{3,2,0,1:T(8,128)S(1)} async-done(((f32[3,16,8,512]{3,2,0,1:T(8,128)}), f32[3,16,8,512]{3,2,0,1:T(8,128)S(1)}, u32[]{:S(2)}, u32[]{:S(2)}) %all-to-all-start) | async-done | bytes 786464 | tf_op jit(solution)/shard_map/all_to_all | solution.py:98
  59.1 1.0 fusion.64
  60.2 1.0 fusion.102
  61.3 1.9 fusion.25
  63.3 0.8 copy-done.1
  64.1 1.1 fusion.29
  65.4 0.7 copy-done.5
  66.1 1.1 convolution_add_fusion.1
  67.3 1.0 fusion.101
  68.5 1.9 fusion.3
  70.4 2.0 fusion.36
  72.9 1.1 fusion.7
  74.0 1.1 fusion.40
  75.4 1.1 convolution_add_fusion.3
  76.5 1.0 fusion.100
  77.7 1.9 fusion.14
  79.8 1.1 fusion.18
  81.1 1.1 convolution_add_fusion
  82.2 1.2 multiply_reduce_fusion.3
  84.1 0.7 copy.248
  86.0 0.7 copy.198
  86.7 4.0 %all-to-all-start.5 = ((f32[2,16,512]{2,0,1:T(2,128)}), f32[2,16,512]{2,0,1:T(2,128)S(1)}, u32[]{:S(2)}, u32[]{:S(2)}) async-start(f32[2,16,512]{2,0,1:T(2,128)} %copy.198), calls=%async_computation.5 | async-start | bytes 131072 | tf_op jit(solution)/shard_map/all_to_all | solution.py:170
  91.5 67.0 %psum.30 = f32[3,4,128]{2,1,0:T(4,128)S(1)} all-reduce(f32[3,4,128]{2,1,0:T(4,128)S(1)} %reshape.136), channel_id=1, replica_groups=mesh['dp'=8,'seq'=16] {'dp','seq'}, use_global_device_ids=true, to_apply=%region_7.8 | all-reduce | flops 1536 | bytes 12288 | tf_op jit(solution)/shard_map/psum | solution.py:189
  160.2 1.0 copy.188
  161.2 0.7 copy.177
  161.9 4.3 %all-to-all-start.2 = ((bf16[16,4,8,128]{3,2,1,0:T(8,128)(2,1)}), bf16[16,4,8,128]{3,2,1,0:T(8,128)(2,1)S(1)}, u32[]{:S(2)}, u32[]{:S(2)}) async-start(bf16[16,4,8,128]{3,2,1,0:T(8,128)(2,1)} %copy.177), calls=%async_computation.2 | async-start | bytes 262144 | tf_op jit(solution)/shard_map/all_to_all | solution.py:153
  166.3 25.2 %psum.31 = f32[2,8,512]{2,0,1:T(2,128)S(1)} all-reduce(f32[2,8,512]{2,0,1:T(2,128)S(1)} %bitcast_reduce_fusion), channel_id=1, replica_groups=mesh['dp'=8,'seq'=16] {'dp'}, use_global_device_ids=true, to_apply=%region_11.12 | all-reduce | flops 8192 | bytes 65536 | tf_op jit(solution)/shard_map/psum | solution.py:192
  192.7 14.6 %all-to-all-start.4 = ((bf16[3,8,16,512]{3,1,0,2:T(8,128)(2,1)}), bf16[3,8,16,512]{3,1,0,2:T(8,128)(2,1)S(1)}, u32[]{:S(2)}, u32[]{:S(2)}) async-start(bf16[3,8,16,512]{3,1,0,2:T(8,128)(2,1)} %copy.188), calls=%async_computation.4 | async-start | bytes 786432 | tf_op jit(solution)/shard_map/all_to_all | solution.py:162
  207.3 0.9 fusion
  208.2 0.8 fusion.66
  209.0 8.0 %all-to-all-done.4 = bf16[3,8,16,512]{3,1,0,2:T(8,128)(2,1)S(1)} async-done(((bf16[3,8,16,512]{3,1,0,2:T(8,128)(2,1)}), bf16[3,8,16,512]{3,1,0,2:T(8,128)(2,1)S(1)}, u32[]{:S(2)}, u32[]{:S(2)}) %all-to-all-start.4) | async-done | bytes 393248 | tf_op jit(solution)/shard_map/all_to_all | solution.py:162
  217.1 0.9 convolution_bitcast_fusion.2
  218.1 1.0 fusion.2
  219.0 136.0 %all-reduce.7.cloned.1.call-done = (f32[128,384]{0,1:T(8,128)}, f32[128,128]{1,0:T(8,128)}) async-done(((f32[128,384]{0,1:T(8,128)}, f32[128,128]{1,0:T(8,128)}), (f32[128,384]{0,1:T(8,128)}, f32[128,128]{1,0:T(8,128)})) %all-reduce.7.cloned.1.call-update) | async-done | bytes 262160 | tf_op jit(solution)/shard_map/psum | solution.py:189
  355.0 0.9 broadcast_multiply_fusion
  356.0 0.8 copy.199
  356.8 0.6 broadcast_multiply_fusion.1
  (89 shorter events, 12.5 us)
Async XLA Ops:
  7.2 13.4 %copy-start = (bf16[1,512,128]{2,1,0:T(8,128)(2,1)S(1)}, bf16[1,512,128]{2,1,0:T(8,128)(2,1)}, u32[]{:S(2)}) copy-start(bf16[1,512,128]{2,1,0:T(8,128)(2,1)} %param.15) | copy-start | bytes 393220
  8.6 10.5 %copy-start.8 = (bf16[128,384]{1,0:T(8,128)(2,1)S(1)}, bf16[128,384]{1,0:T(8,128)(2,1)}, u32[]{:S(2)}) copy-start(bf16[128,384]{1,0:T(8,128)(2,1)} %param.17) | copy-start | bytes 294916
  8.6 16.8 %all-to-all-start.1 = ((f32[16,2,512]{2,1,0:T(2,128)}), f32[16,2,512]{2,1,0:T(2,128)S(1)}, u32[]{:S(2)}, u32[]{:S(2)}) async-start(f32[16,2,512]{2,1,0:T(2,128)} %bitcast.12), calls=%async_computation.1 | async-start | bytes 131072 | tf_op jit(solution)/shard_map/all_to_all | solution.py:88
  18.1 0.7 copy-start.11
  19.2 0.7 copy-start.12
  19.8 0.7 copy-start.13
  20.6 1.2 copy-start.7
  20.6 1.2 copy-start.10
  25.4 13.3 %all-to-all-start.3 = ((f32[16,8,512]{2,1,0:T(8,128)}), f32[16,8,512]{2,1,0:T(8,128)S(1)}, u32[]{:S(2)}, u32[]{:S(2)}) async-start(f32[16,8,512]{2,1,0:T(8,128)} %fusion.70), calls=%async_computation.3 | async-start | bytes 524288 | tf_op jit(solution)/shard_map/all_to_all | solution.py:117
  30.0 0.8 copy-start.6
  30.8 0.8 copy-start.3
  30.8 0.9 copy-start.4
  31.7 11.1 %copy-start.2 = (f32[256,256,1]{1,0,2:T(8,128)S(1)}, f32[256,256,1]{1,0,2:T(8,128)}, u32[]{:S(2)}) copy-start(f32[256,256,1]{1,0,2:T(8,128)} %constant.59) | copy-start | bytes 786436
  38.7 18.8 %all-to-all-start = ((f32[3,16,8,512]{3,2,0,1:T(8,128)}), f32[3,16,8,512]{3,2,0,1:T(8,128)S(1)}, u32[]{:S(2)}, u32[]{:S(2)}) async-start(f32[3,16,8,512]{3,2,0,1:T(8,128)} %fusion.68), calls=%async_computation | async-start | bytes 1572864 | tf_op jit(solution)/shard_map/all_to_all | solution.py:98
  63.2 1.0 copy-start.1
  65.3 0.8 copy-start.5
  86.7 75.3 %all-to-all-start.5 = ((f32[2,16,512]{2,0,1:T(2,128)}), f32[2,16,512]{2,0,1:T(2,128)S(1)}, u32[]{:S(2)}, u32[]{:S(2)}) async-start(f32[2,16,512]{2,0,1:T(2,128)} %copy.198), calls=%async_computation.5 | async-start | bytes 131072 | tf_op jit(solution)/shard_map/all_to_all | solution.py:170
  161.9 30.8 %all-to-all-start.2 = ((bf16[16,4,8,128]{3,2,1,0:T(8,128)(2,1)}), bf16[16,4,8,128]{3,2,1,0:T(8,128)(2,1)S(1)}, u32[]{:S(2)}, u32[]{:S(2)}) async-start(bf16[16,4,8,128]{3,2,1,0:T(8,128)(2,1)} %copy.177), calls=%async_computation.2 | async-start | bytes 262144 | tf_op jit(solution)/shard_map/all_to_all | solution.py:153
  192.7 24.4 %all-to-all-start.4 = ((bf16[3,8,16,512]{3,1,0,2:T(8,128)(2,1)}), bf16[3,8,16,512]{3,1,0,2:T(8,128)(2,1)S(1)}, u32[]{:S(2)}, u32[]{:S(2)}) async-start(bf16[3,8,16,512]{3,1,0,2:T(8,128)(2,1)} %copy.188), calls=%async_computation.4 | async-start | bytes 786432 | tf_op jit(solution)/shard_map/all_to_all | solution.py:162
  207.3 147.7 %all-reduce.7.cloned.1.call-start = ((), (), s32[]{:S(2)}) async-start(), calls=%async_computation.6 | async-start | bytes 524288 | tf_op jit(solution)/shard_map/psum | solution.py:189
  356.0 0.8 copy-start.9
Sparse Core Ops, SparseCore 0:
  218.2 136.7 all-reduce.6
where the time goes:
time: 365 us; the launch traced here: 364 us
  waiting for transfers between devices  168 us (46%)
  blocking collectives  92.2 us (25%)
  starting transfers between devices  41.2 us (11%)
  matrix products  28.5 us (8%)
  between operations  14.5 us (4%)
  local copies, waits for them, and re-layouts  13.5 us (4%)
  other arithmetic  6.89 us (2%)
    psum x1, waiting for transfers between devices, shards(): lax.psum((local_w_in, local_w_out, small_full), ('dp', 'seq'))  136 us
    psum x1, blocking collectives, shards(): lax.psum((local_w_in, local_w_out, small_full), ('dp', 'seq'))  67 us
    psum x1, blocking collectives, shards(): fg_blocks = lax.psum(fg_blocks, 'dp')  25.2 us
    all_to_all x1, starting transfers between devices, shards(): dp_blocks = lax.all_to_all(dp_blocks, 'seq', 2, 2, tiled=True)  14.6 us
    all_to_all x1, waiting for transfers between devices, shards(): lax.all_to_all(proj_blk.reshape(3, seq_n, per, block), 'seq', 1, 1, tiled...  13.9 us
    all_to_all x1, starting transfers between devices, shards(): rows_got = lax.all_to_all(rows_sent, 'seq', 0, 0, tiled=True)  9.43 us
    unnamed x37, local copies, waits for them, and re-layouts  8.79 us
    dot_general x5, matrix products, spectrum(): return jnp.einsum('kcm,mj->kcj', cat, tab['fwd2'], precision=HIGHEST)  8.23 us
  transfers between devices with their start and end apart: 7, of which 5 were waited for; matrix products, arithmetic and copies ran while one was open for 3% of the time, Pallas kernels for 0%

commit v1 on v0

--- a/solution.py
+++ b/solution.py
@@ -7,6 +7,9 @@
 
 HIGHEST = lax.Precision.HIGHEST
 LANES = 128
+sums_all_direct = lambda v0, dev_axis, row_axis: jax.lax.psum(
+    jax.lax.psum(v0, dev_axis), axis_name=row_axis
+)
 
 
 def dft_tables(length):
@@ -186,8 +189,8 @@
     )
     small_full = jnp.zeros((3, 4, seq_n, per), jnp.float32)
     small_full = lax.dynamic_update_slice(small_full, small, (0, 0, me, 0))
-    grad_w_in, grad_w_out, small_full = lax.psum(
-        (local_w_in, local_w_out, small_full), ("dp", "seq")
+    grad_w_in, grad_w_out, small_full = sums_all_direct(
+        (local_w_in, local_w_out, small_full), dev_axis="seq", row_axis="dp"
     )
     fg_blocks = lax.psum(fg_blocks, "dp")
     small_full = small_full.reshape(3, 4, width)

time: 365 us -> 441 us (1.21)
  waiting for transfers between devices: 168 us -> 234 us
  starting transfers between devices: 41.2 us -> 46.4 us
    psum x1 -> x2, waiting for transfers between devices: 136 us -> 201 us  [the longest x1 129 us: jax.lax.psum(v0, dev_axis)]
    all_to_all x1, starting transfers between devices: 4.33 us -> 9.25 us  [shards(): prod_blocks = lax.all_to_all(prod_blocks, 'seq', 0, 0, tiled=True)]
  transfers between devices with their start and end apart: 7 -> 8, of which waited for: 5 -> 6; matrix products, arithmetic and copies ran while one was open for 3% -> 3% of each run, Pallas kernels for 0% -> 0%
where the time goes in v1:
time: 441 us; the launch traced here: 436 us
  waiting for transfers between devices  234 us (53%)
  blocking collectives  92.4 us (21%)
  starting transfers between devices  46.4 us (11%)
  matrix products  28.5 us (6%)
  between operations  14.6 us (3%)
  local copies, waits for them, and re-layouts  13.5 us (3%)
  other arithmetic  6.89 us (2%)
    psum x1, waiting for transfers between devices, jax.lax.psum(v0, dev_axis)  129 us
    psum x1, waiting for transfers between devices, jax.lax.psum(jax.lax.psum(v0, dev_axis), axis_name=row_axis)  71.8 us
    psum x1, blocking collectives, jax.lax.psum(v0, dev_axis)  65.2 us
    psum x1, blocking collectives, jax.lax.psum(jax.lax.psum(v0, dev_axis), axis_name=row_axis)  27.2 us
    all_to_all x1, starting transfers between devices, shards(): dp_blocks = lax.all_to_all(dp_blocks, 'seq', 2, 2, tiled=True)  14.9 us
    all_to_all x1, waiting for transfers between devices, shards(): lax.all_to_all(proj_blk.reshape(3, seq_n, per, block), 'seq', 1, 1, tiled...  13.9 us
    all_to_all x1, starting transfers between devices, shards(): rows_got = lax.all_to_all(rows_sent, 'seq', 0, 0, tiled=True)  9.43 us
    all_to_all x1, starting transfers between devices, shards(): prod_blocks = lax.all_to_all(prod_blocks, 'seq', 0, 0, tiled=True)  9.25 us
  transfers between devices with their start and end apart: 8, of which 6 were waited for; matrix products, arithmetic and copies ran while one was open for 3% of the time, Pallas kernels for 0%

profile of v1, /device:TPU:1, one launch (start us, length us, event | category | flops | bytes accessed | tf_op | source)
XLA Modules:
  0.0 436.0 jit_solution(1665334850825399937)
XLA Ops:
  7.2 0.8 maximum_bitcast_fusion
  8.0 0.6 broadcast_in_dim.16
  8.6 9.4 %all-to-all-start.1 = ((f32[16,2,512]{2,1,0:T(2,128)}), f32[16,2,512]{2,1,0:T(2,128)S(1)}, u32[]{:S(2)}, u32[]{:S(2)}) async-start(f32[16,2,512]{2,1,0:T(2,128)} %bitcast.12), calls=%async_computation.1 | async-start | bytes 131072 | tf_op jit(solution)/shard_map/all_to_all | solution.py:91
  18.1 0.7 copy-done.11
  20.6 1.2 fusion.68
  21.8 0.9 fusion.70
  22.7 2.7 all-to-all-done.1
  25.4 4.6 %all-to-all-start.3 = ((f32[16,8,512]{2,1,0:T(8,128)}), f32[16,8,512]{2,1,0:T(8,128)S(1)}, u32[]{:S(2)}, u32[]{:S(2)}) async-start(f32[16,8,512]{2,1,0:T(8,128)} %fusion.70), calls=%async_computation.3 | async-start | bytes 524288 | tf_op jit(solution)/shard_map/all_to_all | solution.py:120
  30.0 0.8 copy-done.6
  31.8 6.9 %all-to-all-done.3 = f32[16,8,512]{2,1,0:T(8,128)S(1)} async-done(((f32[16,8,512]{2,1,0:T(8,128)}), f32[16,8,512]{2,1,0:T(8,128)S(1)}, u32[]{:S(2)}, u32[]{:S(2)}) %all-to-all-start.3) | async-done | bytes 262176 | tf_op jit(solution)/shard_map/all_to_all | solution.py:120
  38.7 4.2 all-to-all-start
  43.6 13.9 %all-to-all-done = f32[3,16,8,512]{3,2,0,1:T(8,128)S(1)} async-done(((f32[3,16,8,512]{3,2,0,1:T(8,128)}), f32[3,16,8,512]{3,2,0,1:T(8,128)S(1)}, u32[]{:S(2)}, u32[]{:S(2)}) %all-to-all-start) | async-done | bytes 786464 | tf_op jit(solution)/shard_map/all_to_all | solution.py:101
  59.1 1.0 fusion.64
  60.2 1.0 fusion.102
  61.3 1.9 fusion.25
  63.3 0.8 copy-done.1
  64.1 1.1 fusion.29
  65.4 0.7 copy-done.5
  66.1 1.1 convolution_add_fusion.1
  67.3 1.0 fusion.101
  68.5 1.9 fusion.3
  70.4 2.0 fusion.36
  72.9 1.1 fusion.7
  74.0 1.1 fusion.40
  75.4 1.1 convolution_add_fusion.3
  76.5 1.0 fusion.100
  77.7 1.9 fusion.14
  79.8 1.1 fusion.18
  81.1 1.1 convolution_add_fusion
  82.2 1.2 multiply_reduce_fusion.3
  84.1 0.7 copy.248
  86.0 0.7 copy.198
  86.7 4.0 all-to-all-start.5
  91.9 65.2 %psum.53 = f32[3,4,16,8]{3,2,1,0:T(8,128)S(1)} all-reduce(f32[3,4,16,8]{3,2,1,0:T(8,128)S(1)} %dynamic_update_slice.3), channel_id=1, replica_groups=mesh['dp'=8,'seq'=16] {'seq'}, use_global_device_ids=true, to_apply=%region_9.10 | all-reduce | flops 1536 | bytes 12288 | tf_op jit(solution)/shard_map/psum | solution.py:11
  157.3 1.0 copy.188
  158.3 0.7 copy.177
  159.0 9.3 %all-to-all-start.2 = ((bf16[16,4,8,128]{3,2,1,0:T(8,128)(2,1)}), bf16[16,4,8,128]{3,2,1,0:T(8,128)(2,1)S(1)}, u32[]{:S(2)}, u32[]{:S(2)}) async-start(bf16[16,4,8,128]{3,2,1,0:T(8,128)(2,1)} %copy.177), calls=%async_computation.2 | async-start | bytes 262144 | tf_op jit(solution)/shard_map/all_to_all | solution.py:156
  168.3 27.2 %all-reduce.5 = (f32[3,4,128]{2,1,0:T(4,128)S(1)}, f32[2,8,512]{2,0,1:T(2,128)S(1)}) all-reduce(f32[3,4,128]{2,1,0:T(4,128)S(1)} %reshape.136, f32[2,8,512]{2,0,1:T(2,128)S(1)} %bitcast_reduce_fusion), channel_id=1, replica_groups=mesh['dp'=8,'seq'=16] {'dp'}, use_global_device_ids=true, to_apply=%region_10.11 | all-reduce | flops 9728 | bytes 77824 | tf_op jit(solution)/shard_map/psum | solution.py:10
  195.5 14.9 %all-to-all-start.4 = ((bf16[3,8,16,512]{3,1,0,2:T(8,128)(2,1)}), bf16[3,8,16,512]{3,1,0,2:T(8,128)(2,1)S(1)}, u32[]{:S(2)}, u32[]{:S(2)}) async-start(bf16[3,8,16,512]{3,1,0,2:T(8,128)(2,1)} %copy.188), calls=%async_computation.4 | async-start | bytes 786432 | tf_op jit(solution)/shard_map/all_to_all | solution.py:165
  210.4 0.8 fusion.66
  211.2 8.9 %all-to-all-done.4 = bf16[3,8,16,512]{3,1,0,2:T(8,128)(2,1)S(1)} async-done(((bf16[3,8,16,512]{3,1,0,2:T(8,128)(2,1)}), bf16[3,8,16,512]{3,1,0,2:T(8,128)(2,1)S(1)}, u32[]{:S(2)}, u32[]{:S(2)}) %all-to-all-start.4) | async-done | bytes 393248 | tf_op jit(solution)/shard_map/all_to_all | solution.py:165
  220.2 0.9 convolution_bitcast_fusion.2
  223.5 0.9 fusion
  224.4 129.5 %all-reduce.10.cloned.1.call-done = (f32[128,384]{0,1:T(8,128)}, f32[128,128]{1,0:T(8,128)}) async-done(((f32[128,384]{0,1:T(8,128)}, f32[128,128]{1,0:T(8,128)}), (f32[128,384]{0,1:T(8,128)}, f32[128,128]{1,0:T(8,128)})) %all-reduce.10.cloned.1.call-update) | async-done | bytes 262160 | tf_op jit(solution)/shard_map/psum | solution.py:11
  353.9 1.0 fusion.2
  354.9 71.8 %all-reduce.12.cloned.1.call-done = (f32[128,384]{0,1:T(8,128)}, f32[128,128]{1,0:T(8,128)}) async-done(((f32[128,384]{0,1:T(8,128)}, f32[128,128]{1,0:T(8,128)}), (f32[128,384]{0,1:T(8,128)}, f32[128,128]{1,0:T(8,128)})) %all-reduce.12.cloned.1.call-update) | async-done | bytes 262160 | tf_op jit(solution)/shard_map/psum | solution.py:10
  426.7 0.9 broadcast_multiply_fusion
  427.7 0.8 copy.199
  (92 shorter events, 13.2 us)
Async XLA Ops:
  7.2 13.4 %copy-start = (bf16[1,512,128]{2,1,0:T(8,128)(2,1)S(1)}, bf16[1,512,128]{2,1,0:T(8,128)(2,1)}, u32[]{:S(2)}) copy-start(bf16[1,512,128]{2,1,0:T(8,128)(2,1)} %param.15) | copy-start | bytes 393220
  8.6 10.5 %copy-start.8 = (bf16[128,384]{1,0:T(8,128)(2,1)S(1)}, bf16[128,384]{1,0:T(8,128)(2,1)}, u32[]{:S(2)}) copy-start(bf16[128,384]{1,0:T(8,128)(2,1)} %param.17) | copy-start | bytes 294916
  8.6 16.8 %all-to-all-start.1 = ((f32[16,2,512]{2,1,0:T(2,128)}), f32[16,2,512]{2,1,0:T(2,128)S(1)}, u32[]{:S(2)}, u32[]{:S(2)}) async-start(f32[16,2,512]{2,1,0:T(2,128)} %bitcast.12), calls=%async_computation.1 | async-start | bytes 131072 | tf_op jit(solution)/shard_map/all_to_all | solution.py:91
  18.1 0.7 copy-start.11
  19.2 0.7 copy-start.12
  19.8 0.7 copy-start.13
  20.6 1.2 copy-start.7
  20.6 1.2 copy-start.10
  25.4 13.3 %all-to-all-start.3 = ((f32[16,8,512]{2,1,0:T(8,128)}), f32[16,8,512]{2,1,0:T(8,128)S(1)}, u32[]{:S(2)}, u32[]{:S(2)}) async-start(f32[16,8,512]{2,1,0:T(8,128)} %fusion.70), calls=%async_computation.3 | async-start | bytes 524288 | tf_op jit(solution)/shard_map/all_to_all | solution.py:120
  30.0 0.8 copy-start.6
  30.8 0.8 copy-start.3
  30.8 0.9 copy-start.4
  31.8 11.1 %copy-start.2 = (f32[256,256,1]{1,0,2:T(8,128)S(1)}, f32[256,256,1]{1,0,2:T(8,128)}, u32[]{:S(2)}) copy-start(f32[256,256,1]{1,0,2:T(8,128)} %constant.59) | copy-start | bytes 786436
  38.7 18.8 %all-to-all-start = ((f32[3,16,8,512]{3,2,0,1:T(8,128)}), f32[3,16,8,512]{3,2,0,1:T(8,128)S(1)}, u32[]{:S(2)}, u32[]{:S(2)}) async-start(f32[3,16,8,512]{3,2,0,1:T(8,128)} %fusion.68), calls=%async_computation | async-start | bytes 1572864 | tf_op jit(solution)/shard_map/all_to_all | solution.py:101
  63.2 1.0 copy-start.1
  65.3 0.8 copy-start.5
  86.7 72.4 %all-to-all-start.5 = ((f32[2,16,512]{2,0,1:T(2,128)}), f32[2,16,512]{2,0,1:T(2,128)S(1)}, u32[]{:S(2)}, u32[]{:S(2)}) async-start(f32[2,16,512]{2,0,1:T(2,128)} %copy.198), calls=%async_computation.5 | async-start | bytes 131072 | tf_op jit(solution)/shard_map/all_to_all | solution.py:173
  159.0 36.5 %all-to-all-start.2 = ((bf16[16,4,8,128]{3,2,1,0:T(8,128)(2,1)}), bf16[16,4,8,128]{3,2,1,0:T(8,128)(2,1)S(1)}, u32[]{:S(2)}, u32[]{:S(2)}) async-start(bf16[16,4,8,128]{3,2,1,0:T(8,128)(2,1)} %copy.177), calls=%async_computation.2 | async-start | bytes 262144 | tf_op jit(solution)/shard_map/all_to_all | solution.py:156
  195.5 24.6 %all-to-all-start.4 = ((bf16[3,8,16,512]{3,1,0,2:T(8,128)(2,1)}), bf16[3,8,16,512]{3,1,0,2:T(8,128)(2,1)S(1)}, u32[]{:S(2)}, u32[]{:S(2)}) async-start(bf16[3,8,16,512]{3,1,0,2:T(8,128)(2,1)} %copy.188), calls=%async_computation.4 | async-start | bytes 786432 | tf_op jit(solution)/shard_map/all_to_all | solution.py:165
  210.4 143.5 %all-reduce.10.cloned.1.call-start = ((), (), s32[]{:S(2)}) async-start(), calls=%async_computation.6 | async-start | bytes 524288 | tf_op jit(solution)/shard_map/psum | solution.py:11
  221.2 205.6 %all-reduce.12.cloned.1.call-start = ((), (), s32[]{:S(2)}) async-start(), calls=%async_computation.7 | async-start | bytes 524288 | tf_op jit(solution)/shard_map/psum | solution.py:10
  427.7 0.8 copy-start.9
Sparse Core Ops, SparseCore 0:
  221.3 132.5 all-reduce.9
  356.6 70.0 all-reduce.11
